TPU v7x, 256 devices: a whole 4x4x8 slice. The times are simulated.
256 devices in a mesh: rows: 32 (over y, z), tensor: 8 (over x, core).
Axes of the slice: x: 4, y: 4, z: 8, core: 2. Of those that a mesh axis runs over, the one named last changes fastest.
Arguments:
- token_ids: int32 [256, 4], replicated, may hold values from 0 to 65535
- cache_lengths: int32 [256], P('rows'), may hold values from 160 to 1280, as said below
- doc_ids: int32 [256], replicated, may hold values from 0 to 31
- embed_table: bfloat16 [65536, 8192], P('tensor', 'rows'), may hold values from -10.5 to 10.5
- cache_keys: bfloat16 [256, 1280, 1024], P('rows', None, 'tensor'), may hold values from -700 to 700
- cache_values: bfloat16 [256, 1280, 1024], P('rows', None, 'tensor'), may hold values from -6 to 6
- decode_gain: float32 [8192], P('rows'), may hold values from 0.1 to 1.9
- decode_query: bfloat16 [8192, 8192], P('rows', 'tensor'), may hold values from -0.0625 to 0.0625
- decode_key: bfloat16 [8192, 1024], P('rows', 'tensor'), may hold values from -0.0625 to 0.0625
- decode_value: bfloat16 [8192, 1024], P('rows', 'tensor'), may hold values from -0.0625 to 0.0625
- decode_out: bfloat16 [8192, 8192], P('tensor', 'rows'), may hold values from -0.0625 to 0.0625
- reduce_gain: float32 [8192], P('rows'), may hold values from 0.8 to 10
- reduce_query: bfloat16 [8192, 8192], P('rows', 'tensor'), may hold values from -0.0625 to 0.0625
- reduce_key: bfloat16 [8192, 1024], P('rows', 'tensor'), may hold values from -0.0625 to 0.0625
- reduce_value: bfloat16 [8192, 1024], P('rows', 'tensor'), may hold values from -0.0625 to 0.0625
- reduce_out: bfloat16 [8192, 8192], P('tensor', 'rows'), may hold values from -0.0625 to 0.0625
Outputs:
- reduced: bfloat16 [1024, 8192], P(None, 'rows')
Inputs may be any that keep to these rules, and one draw needn't show every extreme that they name: Passage row c holds cache entries at positions below cache_lengths[c]; one row in every draw has a full cache of 1280.
All inputs are finite; a program needn't handle non-finite values.
Results may differ from a plain program's by a relative error of at most 0.035.
The roundings to bfloat16 on the way count: a program that leaves them out, or rounds other values in their place, can miss the bound.
Values may be sent and summed in bfloat16 or wider, within the bound.
A program may use at most 64 MiB of HBM per device.

v0:
```python
import jax
import jax.numpy as jnp
from jax import lax
from jax.sharding import PartitionSpec as P

D = 8192
HEAD_DIM = 128
EPSILON = 1e-05
ROPE_BASE = 500000.0


def rotate(vectors, positions):
    half_dim = vectors.shape[-1] // 2
    frequencies = ROPE_BASE ** (-2.0 * jnp.arange(half_dim, dtype=jnp.float32) / vectors.shape[-1])
    angles = positions.astype(jnp.float32)[..., None] * frequencies
    cosine = jnp.cos(angles)
    sine_part = jnp.sin(angles)
    lower_half = vectors[..., :half_dim]
    upper_half = vectors[..., half_dim:]
    return jnp.concatenate(
        [
            lower_half * cosine - upper_half * sine_part,
            upper_half * cosine + lower_half * sine_part,
        ],
        axis=-1,
    )


def width_total(partial_value):
    return lax.psum(partial_value, "tensor")


def row_scale(squares):
    summed = lax.psum(squares, "rows")
    return lax.rsqrt(summed / D + EPSILON)


def head_terms(normed, matrices):
    return lax.psum_scatter(
        jnp.concatenate(
            [jnp.dot(normed, matrix, preferred_element_type=jnp.float32) for matrix in matrices],
            axis=1,
        ),
        "rows",
        scatter_dimension=0,
        tiled=True,
    )


def head_mix(attended, matrix):
    return jnp.dot(
        lax.all_gather(attended, "rows", axis=0, tiled=True),
        matrix,
        preferred_element_type=jnp.float32,
    )


def per_device(
    token_ids,
    cache_lengths,
    doc_ids,
    embed_table,
    cache_keys,
    cache_values,
    decode_gain,
    decode_query,
    decode_key,
    decode_value,
    decode_out,
    reduce_gain,
    reduce_query,
    reduce_key,
    reduce_value,
    reduce_out,
):
    step_count = token_ids.shape[1]
    passage_count = token_ids.shape[0]
    token_count = passage_count * step_count
    own_passages = cache_lengths.shape[0]
    own_tokens = own_passages * step_count
    row_first = lax.axis_index("rows") * own_tokens
    query_cols = decode_query.shape[1]
    kv_cols = decode_key.shape[1]
    local_heads = query_cols // HEAD_DIM
    local_kv = kv_cols // HEAD_DIM
    group_size = local_heads // local_kv
    score_scale = HEAD_DIM ** (-0.5)
    step_ids = jnp.arange(step_count, dtype=jnp.int32)
    vocab_part = embed_table.shape[0]
    local_ids = token_ids.reshape(token_count) - lax.axis_index("tensor") * vocab_part
    inside = (local_ids >= 0) & (local_ids < vocab_part)
    picked = jnp.take(embed_table, jnp.clip(local_ids, 0, vocab_part - 1), axis=0)
    picked = jnp.where(inside[:, None], picked.astype(jnp.float32), 0.0)
    embedded = width_total(picked)
    dec_scale = row_scale(jnp.sum(embedded * embedded, axis=1))
    normed = (embedded * decode_gain[None, :]).astype(jnp.bfloat16)
    projected = head_terms(normed, (decode_query, decode_key, decode_value))
    projected = projected * lax.dynamic_slice_in_dim(dec_scale, row_first, own_tokens, 0)[:, None]
    positions = (cache_lengths[:, None] + step_ids[None, :]).reshape(own_tokens, 1)
    queries = rotate(
        projected[:, :query_cols].reshape(own_tokens, local_heads, HEAD_DIM), positions
    ).astype(jnp.bfloat16)
    keys_new = rotate(
        projected[:, query_cols : query_cols + kv_cols].reshape(own_tokens, local_kv, HEAD_DIM),
        positions,
    ).astype(jnp.bfloat16)
    values_new = projected[:, query_cols + kv_cols :].astype(jnp.bfloat16)
    queries = queries.reshape(own_passages, step_count, local_kv, group_size, HEAD_DIM)
    keys_new = keys_new.reshape(own_passages, step_count, local_kv, HEAD_DIM)
    values_new = values_new.reshape(own_passages, step_count, local_kv, HEAD_DIM)
    capacity = cache_keys.shape[1]
    keys_old = cache_keys.reshape(own_passages, capacity, local_kv, HEAD_DIM)
    values_old = cache_values.reshape(own_passages, capacity, local_kv, HEAD_DIM)
    new_scores = (
        jnp.einsum("rskgd,rtkd->rskgt", queries, keys_new, preferred_element_type=jnp.float32)
        * score_scale
    )
    causal = step_ids[None, :] <= step_ids[:, None]
    new_scores = jnp.where(causal[None, :, None, None, :], new_scores, -jnp.inf)
    old_scores = (
        jnp.einsum("rskgd,rckd->rskgc", queries, keys_old, preferred_element_type=jnp.float32)
        * score_scale
    )
    slot_ids = jnp.arange(capacity, dtype=jnp.int32)
    live_mask = slot_ids[None, :] < cache_lengths[:, None]
    old_scores = jnp.where(live_mask[:, None, None, None, :], old_scores, -jnp.inf)
    highest = jnp.maximum(jnp.max(old_scores, axis=-1), jnp.max(new_scores, axis=-1))
    old_exp = jnp.exp(old_scores - highest[..., None])
    new_exp = jnp.exp(new_scores - highest[..., None])
    summed = jnp.sum(old_exp, axis=-1) + jnp.sum(new_exp, axis=-1)
    old_weights = (old_exp / summed[..., None]).astype(jnp.bfloat16)
    new_weights = (new_exp / summed[..., None]).astype(jnp.bfloat16)
    attended = jnp.einsum(
        "rskgc,rckd->rskgd", old_weights, values_old, preferred_element_type=jnp.float32
    )
    attended = attended + jnp.einsum(
        "rskgt,rtkd->rskgd", new_weights, values_new, preferred_element_type=jnp.float32
    )
    attended = attended.reshape(own_tokens, query_cols).astype(jnp.bfloat16)
    partial_value = head_mix(attended, decode_out)
    summary = (embedded + width_total(partial_value)).astype(jnp.bfloat16)
    summary_wide = summary.astype(jnp.float32)
    red_scale = row_scale(jnp.sum(summary_wide * summary_wide, axis=1))
    normed_red = (summary_wide * reduce_gain[None, :]).astype(jnp.bfloat16)
    passage_index = jnp.arange(passage_count, dtype=jnp.int32)
    earlier = jnp.sum(
        (
            (doc_ids[None, :] == doc_ids[:, None])
            & (passage_index[None, :] < passage_index[:, None])
        ).astype(jnp.int32),
        axis=1,
    )
    doc_positions = (earlier[:, None] * step_count + step_ids[None, :]).reshape(token_count, 1)
    doc_tokens = (doc_ids[:, None] + jnp.zeros_like(step_ids)[None, :]).reshape(token_count)
    own_positions = lax.dynamic_slice_in_dim(doc_positions, row_first, own_tokens, 0)
    own_scale = lax.dynamic_slice_in_dim(red_scale, row_first, own_tokens, 0)[:, None]
    projected = head_terms(normed_red, (reduce_query, reduce_key, reduce_value)) * own_scale
    queries_red = rotate(
        projected[:, :query_cols].reshape(own_tokens, local_heads, HEAD_DIM), own_positions
    ).astype(jnp.bfloat16)
    keys_own = (
        rotate(
            projected[:, query_cols : query_cols + kv_cols].reshape(own_tokens, local_kv, HEAD_DIM),
            own_positions,
        )
        .astype(jnp.bfloat16)
        .reshape(own_tokens, kv_cols)
    )
    values_own = projected[:, query_cols + kv_cols :].astype(jnp.bfloat16)
    keys_red, values_red = (
        lax.all_gather(keys_own, "rows", axis=0, tiled=True),
        lax.all_gather(values_own, "rows", axis=0, tiled=True),
    )
    queries_red = queries_red.reshape(own_tokens, local_kv, group_size, HEAD_DIM)
    keys_red = keys_red.reshape(token_count, local_kv, HEAD_DIM)
    values_red = values_red.reshape(token_count, local_kv, HEAD_DIM)
    token_index = jnp.arange(token_count, dtype=jnp.int32)
    own_index = row_first + jnp.arange(own_tokens, dtype=jnp.int32)
    own_docs = lax.dynamic_slice_in_dim(doc_tokens, row_first, own_tokens, 0)
    allowed = (own_docs[:, None] == doc_tokens[None, :]) & (
        token_index[None, :] <= own_index[:, None]
    )
    red_scores = (
        jnp.einsum("tkgd,ukd->tkgu", queries_red, keys_red, preferred_element_type=jnp.float32)
        * score_scale
    )
    red_scores = jnp.where(allowed[:, None, None, :], red_scores, -jnp.inf)
    red_high = jnp.max(red_scores, axis=-1)
    red_exp = jnp.exp(red_scores - red_high[..., None])
    red_weights = (red_exp / jnp.sum(red_exp, axis=-1)[..., None]).astype(jnp.bfloat16)
    red_out = jnp.einsum(
        "tkgu,ukd->tkgd", red_weights, values_red, preferred_element_type=jnp.float32
    )
    red_out = red_out.reshape(own_tokens, query_cols).astype(jnp.bfloat16)
    return (summary_wide + width_total(head_mix(red_out, reduce_out))).astype(jnp.bfloat16)


def solution(mesh):
    return jax.shard_map(
        per_device,
        mesh=mesh,
        in_specs=(
            P(),
            P("rows"),
            P(),
            P("tensor", "rows"),
            P("rows", None, "tensor"),
            P("rows", None, "tensor"),
            P("rows"),
            P("rows", "tensor"),
            P("rows", "tensor"),
            P("rows", "tensor"),
            P("tensor", "rows"),
            P("rows"),
            P("rows", "tensor"),
            P("rows", "tensor"),
            P("rows", "tensor"),
            P("tensor", "rows"),
        ),
        out_specs=P(None, "rows"),
        check_vma=False,
    )
```

profile of v0, /device:TPU:8, one launch (start us, length us, event | category | flops | bytes accessed | tf_op | source)
XLA Modules:
  0.0 966.4 jit_solution(12764112662389864731)
XLA Ops:
  6.5 0.8 subtract_clamp_fusion
  7.8 0.7 compare_and_fusion.1
  8.8 6.2 gather_fusion
  15.0 1.3 convert_select_fusion
  16.4 70.6 %all-reduce.4.cloned.1.call-done = f32[1024,256]{1,0:T(8,128)} async-done(((f32[1024,256]{1,0:T(8,128)}), f32[1024,256]{1,0:T(8,128)}) %all-reduce.4.cloned.1.call-update) | async-done | bytes 1048592 | tf_op jit(solution)/shard_map/psum | solution.py:30
  87.1 1.4 multiply_reduce_fusion
  88.6 0.8 fusion.72
  90.0 2.8 pad_maximum_fusion
  92.8 5.9 copy.69
  98.8 0.6 copy-done.7
  100.4 63.5 %psum.36 = f32[1024]{0:T(1024)S(1)} all-reduce(f32[1024]{0:T(1024)S(1)} %get-tuple-element.7), channel_id=1, replica_groups=mesh['rows'=32,'tensor'=8] {'rows'}, use_global_device_ids=true, to_apply=%region_3.4 | all-reduce | flops 1024 | bytes 8192 | tf_op jit(solution)/shard_map/psum | solution.py:34
  164.0 160.3 %reduce-scatter.7.cloned.1.call-done = f32[32,1280]{1,0:T(8,128)} async-done(((f32[1024,1280]{1,0:T(8,128)}), f32[32,1280]{1,0:T(8,128)}) %reduce-scatter.7.cloned.1.call-update) | async-done | bytes 163856 | tf_op jit(solution)/shard_map/reduce_scatter | solution.py:39
  324.2 1.0 broadcast_multiply_fusion.1
  325.6 1.1 fusion.69
  328.5 0.6 copy.86
  329.2 75.8 %all-gather.3.cloned.1.call-done = bf16[1024,1024]{1,0:T(8,128)(2,1)} async-done(((bf16[32,1024]{1,0:T(8,128)(2,1)}), bf16[1024,1024]{1,0:T(8,128)(2,1)}) %all-gather.3.cloned.1.call-update) | async-done | bytes 2097168 | tf_op jit(solution)/shard_map/all_gather | solution.py:52
  405.0 3.3 fusion.75
  408.3 66.2 %all-reduce.6.cloned.1.call-done = f32[1024,256]{1,0:T(8,128)} async-done(((f32[1024,256]{1,0:T(8,128)}), f32[1024,256]{1,0:T(8,128)}) %all-reduce.6.cloned.1.call-update) | async-done | bytes 1048592 | tf_op jit(solution)/shard_map/psum | solution.py:30
  474.6 1.8 fusion.22
  476.4 1.8 fusion.32
  478.9 2.8 pad_maximum_fusion.1
  481.6 5.9 copy.71
  488.0 63.5 %psum.38 = f32[1024]{0:T(1024)S(1)} all-reduce(f32[1024]{0:T(1024)S(1)} %get-tuple-element.5), channel_id=1, replica_groups=mesh['rows'=32,'tensor'=8] {'rows'}, use_global_device_ids=true, to_apply=%region_11.12 | all-reduce | flops 1024 | bytes 8192 | tf_op jit(solution)/shard_map/psum | solution.py:34
  551.7 161.6 %reduce-scatter.9.cloned.1.call-done = f32[32,1280]{1,0:T(8,128)} async-done(((f32[1024,1280]{1,0:T(8,128)}), f32[32,1280]{1,0:T(8,128)}) %reduce-scatter.9.cloned.1.call-update) | async-done | bytes 163856 | tf_op jit(solution)/shard_map/reduce_scatter | solution.py:39
  713.2 1.0 broadcast_multiply_fusion
  714.5 47.5 %all_gather.14 = bf16[1024,128]{1,0:T(8,128)(2,1)S(1)} all-gather(bf16[32,128]{1,0:T(8,128)(2,1)S(1)} %pad_maximum_fusion.5), channel_id=1, replica_groups=mesh['rows'=32,'tensor'=8] {'rows'}, dimensions={0}, use_global_device_ids=true | all-gather | bytes 270336 | tf_op jit(solution)/shard_map/all_gather | solution.py:171
  762.1 47.8 %all_gather.13 = bf16[1024,128]{1,0:T(8,128)(2,1)S(1)} all-gather(bf16[32,128]{1,0:T(8,128)(2,1)S(1)} %slice.100), channel_id=1, replica_groups=mesh['rows'=32,'tensor'=8] {'rows'}, dimensions={0}, use_global_device_ids=true | all-gather | bytes 270336 | tf_op jit(solution)/shard_map/all_gather | solution.py:172
  811.2 0.6 copy.85
  811.9 75.9 %all-gather.5.cloned.1.call-done = bf16[1024,1024]{1,0:T(8,128)(2,1)} async-done(((bf16[32,1024]{1,0:T(8,128)(2,1)}), bf16[1024,1024]{1,0:T(8,128)(2,1)}) %all-gather.5.cloned.1.call-update) | async-done | bytes 2097168 | tf_op jit(solution)/shard_map/all_gather | solution.py:52
  887.7 3.4 fusion.76
  891.1 66.3 %all-reduce.8.cloned.1.call-done = f32[1024,256]{1,0:T(8,128)} async-done(((f32[1024,256]{1,0:T(8,128)}), f32[1024,256]{1,0:T(8,128)}) %all-reduce.8.cloned.1.call-update) | async-done | bytes 1048592 | tf_op jit(solution)/shard_map/psum | solution.py:30
  957.4 2.1 fusion.23
  (94 shorter events, 7.5 us)
Async XLA Ops:
  6.5 319.0 %copy-start = (bf16[8,1280,128]{2,1,0:T(8,128)(2,1)S(1)}, bf16[8,1280,128]{2,1,0:T(8,128)(2,1)}, u32[]{:S(2)}) copy-start(bf16[8,1280,128]{2,1,0:T(8,128)(2,1)} %param.20) | copy-start | bytes 7864324
  6.5 80.5 %all-reduce.4.cloned.1.call-start = ((), (), s32[]{:S(2)}) async-start(), calls=%async_computation.2 | async-start | bytes 2097152 | tf_op jit(solution)/shard_map/psum | solution.py:30
  8.8 78.3 %copy-start.9 = (f32[256]{0:T(256)S(1)}, f32[256]{0:T(256)}, u32[]{:S(2)}) copy-start(f32[256]{0:T(256)} %param.22) | copy-start | bytes 3076
  16.4 72.2 %copy-start.1 = (bf16[256,1024]{1,0:T(8,128)(2,1)S(1)}, bf16[256,1024]{1,0:T(8,128)(2,1)}, u32[]{:S(2)}) copy-start(bf16[256,1024]{1,0:T(8,128)(2,1)} %param.23) | copy-start | bytes 1572868
  16.4 307.8 %reduce-scatter.7.cloned.1.call-start = ((), (), s32[]{:S(2)}) async-start(), calls=%async_computation.7 | async-start | bytes 5406720 | tf_op jit(solution)/shard_map/reduce_scatter | solution.py:39
  88.5 0.8 copy-start.2
  88.5 1.1 copy-start.3
  98.7 0.7 copy-start.7
  98.7 1.1 copy-start.8
  98.8 306.2 %all-gather.3.cloned.1.call-start = ((), (), s32[]{:S(2)}) async-start(), calls=%async_computation.3 | async-start | bytes 2162688 | tf_op jit(solution)/shard_map/all_gather | solution.py:52
  325.6 2.3 copy-start.10
  327.9 77.1 %copy-start.11 = (bf16[1024,256]{1,0:T(8,128)(2,1)S(1)}, bf16[1024,256]{1,0:T(8,128)(2,1)}, u32[]{:S(2)}) copy-start(bf16[1024,256]{1,0:T(8,128)(2,1)} %param.26) | copy-start | bytes 1572868
  329.1 145.4 %all-reduce.6.cloned.1.call-start = ((), (), s32[]{:S(2)}) async-start(), calls=%async_computation.4 | async-start | bytes 2097152 | tf_op jit(solution)/shard_map/psum | solution.py:30
  408.3 68.1 %copy-start.6 = (f32[256]{0:T(256)S(1)}, f32[256]{0:T(256)}, u32[]{:S(2)}) copy-start(f32[256]{0:T(256)} %param.27) | copy-start | bytes 3076
  408.3 305.0 %reduce-scatter.9.cloned.1.call-start = ((), (), s32[]{:S(2)}) async-start(), calls=%async_computation.8 | async-start | bytes 5406720 | tf_op jit(solution)/shard_map/reduce_scatter | solution.py:39
  476.3 1.9 copy-start.4
  476.3 2.2 copy-start.5
  487.6 400.1 %all-gather.5.cloned.1.call-start = ((), (), s32[]{:S(2)}) async-start(), calls=%async_computation.5 | async-start | bytes 2162688 | tf_op jit(solution)/shard_map/all_gather | solution.py:52
  811.8 145.6 %all-reduce.8.cloned.1.call-start = ((), (), s32[]{:S(2)}) async-start(), calls=%async_computation.6 | async-start | bytes 2097152 | tf_op jit(solution)/shard_map/psum | solution.py:30
Sparse Core Ops, SparseCore 0:
  16.5 70.5 all-reduce.3
  98.9 225.3 reduce-scatter.6
  329.3 75.6 all-gather.2
  408.4 66.1 all-reduce.5
  487.7 225.4 reduce-scatter.8
  811.9 75.7 all-gather.4
  891.3 66.1 all-reduce.7
where the time goes:
time: 967 us; the launch traced here: 966 us
  waiting for transfers between devices  677 us (70%)
  blocking collectives  222 us (23%)
  local copies, waits for them, and re-layouts  21.6 us (2%)
  other arithmetic  17.9 us (2%)
  between operations  13.9 us (1%)
  matrix products  13.7 us (1%)
    reduce_scatter x2, waiting for transfers between devices, head_terms(): lax.psum_scatter(jnp.concatenate([jnp.dot(normed, matrix, preferred_eleme...  322 us
    psum x3, waiting for transfers between devices, width_total(): return lax.psum(partial_value, 'tensor')  203 us
    all_gather x2, waiting for transfers between devices, head_mix(): lax.all_gather(attended, 'rows', axis=0, tiled=True)  152 us
    psum x2, blocking collectives, row_scale(): summed = lax.psum(squares, 'rows')  127 us
    all_gather x1, blocking collectives, per_device(): lax.all_gather(values_own, 'rows', axis=0, tiled=True)  47.8 us
    all_gather x1, blocking collectives, per_device(): lax.all_gather(keys_own, 'rows', axis=0, tiled=True)  47.5 us
  transfers between devices with their start and end apart: 7, of which 7 were waited for; matrix products, arithmetic and copies ran while one was open for 0% of the time, Pallas kernels for 0%

commit v1 on v0

--- a/solution.py
+++ b/solution.py
@@ -49,7 +49,9 @@
 
 def head_mix(attended, matrix):
     return jnp.dot(
-        lax.all_gather(attended, "rows", axis=0, tiled=True),
+        jnp.concatenate(
+            lax.all_to_all(jnp.stack([attended] * lax.axis_size("rows")), "rows", 0, 0), axis=0
+        ),
         matrix,
         preferred_element_type=jnp.float32,
     )

time: 967 us -> 902 us (0.933)
  waiting for transfers between devices: 677 us -> 525 us
  blocking collectives: 222 us -> 313 us
    all_gather x2 -> x0, waiting for transfers between devices: 152 us -> none  [head_mix(): lax.all_gather(attended, 'rows', axis=0, tiled=True)]
    all_to_all x0 -> x2, blocking collectives: none -> 86.3 us  [head_mix(): lax.all_to_all(jnp.stack([attended] * lax.axis_size('rows')), 'rows', 0, 0)]
  transfers between devices with their start and end apart: 7 -> 5, of which waited for: 7 -> 5; matrix products, arithmetic and copies ran while one was open for 0% -> 0% of each run, Pallas kernels for 0% -> 0%
where the time goes in v1:
time: 902 us; the launch traced here: 901 us
  waiting for transfers between devices  525 us (58%)
  blocking collectives  313 us (35%)
  local copies, waits for them, and re-layouts  20.8 us (2%)
  other arithmetic  17.9 us (2%)
  between operations  13.6 us (2%)
  matrix products  10.5 us (1%)
    reduce_scatter x2, waiting for transfers between devices, head_terms(): lax.psum_scatter(jnp.concatenate([jnp.dot(normed, matrix, preferred_eleme...  321 us
    psum x3, waiting for transfers between devices, width_total(): return lax.psum(partial_value, 'tensor')  203 us
    psum x2, blocking collectives, row_scale(): summed = lax.psum(squares, 'rows')  127 us
    all_to_all x2, blocking collectives, head_mix(): lax.all_to_all(jnp.stack([attended] * lax.axis_size('rows')), 'rows', 0, 0)  86.3 us
    all_gather x1, blocking collectives, per_device(): lax.all_gather(values_own, 'rows', axis=0, tiled=True)  52 us
    all_gather x1, blocking collectives, per_device(): lax.all_gather(keys_own, 'rows', axis=0, tiled=True)  47.6 us
  transfers between devices with their start and end apart: 5, of which 5 were waited for; matrix products, arithmetic and copies ran while one was open for 0% of the time, Pallas kernels for 0%

profile of v1, /device:TPU:8, one launch (start us, length us, event | category | flops | bytes accessed | tf_op | source)
XLA Modules:
  0.0 901.1 jit_solution(7796679217592552730)
XLA Ops:
  6.5 0.8 subtract_clamp_fusion
  7.8 0.7 compare_and_fusion.1
  8.8 6.2 gather_fusion
  15.0 1.3 convert_select_fusion
  16.4 70.6 %all-reduce.4.cloned.1.call-done = f32[1024,256]{1,0:T(8,128)} async-done(((f32[1024,256]{1,0:T(8,128)}), f32[1024,256]{1,0:T(8,128)}) %all-reduce.4.cloned.1.call-update) | async-done | bytes 1048592 | tf_op jit(solution)/shard_map/psum | solution.py:30
  87.1 1.4 multiply_reduce_fusion
  88.6 0.8 fusion.72
  90.0 2.8 pad_maximum_fusion
  92.8 5.9 copy.69
  98.8 0.6 copy-done.7
  100.4 63.7 %psum.36 = f32[1024]{0:T(1024)S(1)} all-reduce(f32[1024]{0:T(1024)S(1)} %get-tuple-element.7), channel_id=1, replica_groups=mesh['rows'=32,'tensor'=8] {'rows'}, use_global_device_ids=true, to_apply=%region_3.4 | all-reduce | flops 1024 | bytes 8192 | tf_op jit(solution)/shard_map/psum | solution.py:34
  164.2 160.2 %reduce-scatter.7.cloned.1.call-done = f32[32,1280]{1,0:T(8,128)} async-done(((f32[1024,1280]{1,0:T(8,128)}), f32[32,1280]{1,0:T(8,128)}) %reduce-scatter.7.cloned.1.call-update) | async-done | bytes 163856 | tf_op jit(solution)/shard_map/reduce_scatter | solution.py:39
  324.4 1.0 broadcast_multiply_fusion.1
  325.7 1.1 fusion.69
  326.8 0.5 fusion.70
  328.0 0.6 fusion.15
  328.9 51.5 %all_to_all.10 = bf16[32,32,1024]{2,1,0:T(8,128)(2,1)S(1)} all-to-all(bf16[32,32,1024]{2,1,0:T(8,128)(2,1)S(1)} %stack.4), channel_id=1, replica_groups=mesh['rows'=32,'tensor'=8] {'rows'}, dimensions={0} | all-to-all | bytes 4194304 | tf_op jit(solution)/shard_map/all_to_all | solution.py:53
  380.4 1.7 fusion.75
  382.2 66.6 %all-reduce.6.cloned.1.call-done = f32[1024,256]{1,0:T(8,128)} async-done(((f32[1024,256]{1,0:T(8,128)}), f32[1024,256]{1,0:T(8,128)}) %all-reduce.6.cloned.1.call-update) | async-done | bytes 1048592 | tf_op jit(solution)/shard_map/psum | solution.py:30
  448.8 1.8 fusion.22
  450.6 1.8 fusion.32
  453.1 2.8 pad_maximum_fusion.1
  455.9 5.9 copy.71
  462.3 63.7 %psum.38 = f32[1024]{0:T(1024)S(1)} all-reduce(f32[1024]{0:T(1024)S(1)} %get-tuple-element.5), channel_id=1, replica_groups=mesh['rows'=32,'tensor'=8] {'rows'}, use_global_device_ids=true, to_apply=%region_11.12 | all-reduce | flops 1024 | bytes 8192 | tf_op jit(solution)/shard_map/psum | solution.py:34
  526.1 161.2 %reduce-scatter.9.cloned.1.call-done = f32[32,1280]{1,0:T(8,128)} async-done(((f32[1024,1280]{1,0:T(8,128)}), f32[32,1280]{1,0:T(8,128)}) %reduce-scatter.9.cloned.1.call-update) | async-done | bytes 163856 | tf_op jit(solution)/shard_map/reduce_scatter | solution.py:39
  687.3 1.0 broadcast_multiply_fusion
  688.6 47.6 %all_gather.7 = bf16[1024,128]{1,0:T(8,128)(2,1)S(1)} all-gather(bf16[32,128]{1,0:T(8,128)(2,1)S(1)} %pad_maximum_fusion.5), channel_id=1, replica_groups=mesh['rows'=32,'tensor'=8] {'rows'}, dimensions={0}, use_global_device_ids=true | all-gather | bytes 270336 | tf_op jit(solution)/shard_map/all_gather | solution.py:173
  736.4 52.0 %all_gather.6 = bf16[1024,128]{1,0:T(8,128)(2,1)S(1)} all-gather(bf16[32,128]{1,0:T(8,128)(2,1)S(1)} %slice.100), channel_id=1, replica_groups=mesh['rows'=32,'tensor'=8] {'rows'}, dimensions={0}, use_global_device_ids=true | all-gather | bytes 270336 | tf_op jit(solution)/shard_map/all_gather | solution.py:174
  789.9 34.8 %all_to_all.11 = bf16[32,32,1024]{2,1,0:T(8,128)(2,1)S(1)} all-to-all(bf16[32,32,1024]{2,1,0:T(8,128)(2,1)S(1)} %stack.5), channel_id=1, replica_groups=mesh['rows'=32,'tensor'=8] {'rows'}, dimensions={0} | all-to-all | bytes 4194304 | tf_op jit(solution)/shard_map/all_to_all | solution.py:53
  824.6 1.7 fusion.76
  826.4 66.1 %all-reduce.8.cloned.1.call-done = f32[1024,256]{1,0:T(8,128)} async-done(((f32[1024,256]{1,0:T(8,128)}), f32[1024,256]{1,0:T(8,128)}) %all-reduce.8.cloned.1.call-update) | async-done | bytes 1048592 | tf_op jit(solution)/shard_map/psum | solution.py:30
  892.5 2.1 fusion.23
  (94 shorter events, 6.8 us)
Async XLA Ops:
  6.5 319.2 %copy-start = (bf16[8,1280,128]{2,1,0:T(8,128)(2,1)S(1)}, bf16[8,1280,128]{2,1,0:T(8,128)(2,1)}, u32[]{:S(2)}) copy-start(bf16[8,1280,128]{2,1,0:T(8,128)(2,1)} %param.20) | copy-start | bytes 7864324
  6.5 80.5 %all-reduce.4.cloned.1.call-start = ((), (), s32[]{:S(2)}) async-start(), calls=%async_computation.4 | async-start | bytes 2097152 | tf_op jit(solution)/shard_map/psum | solution.py:30
  8.8 78.3 %copy-start.9 = (f32[256]{0:T(256)S(1)}, f32[256]{0:T(256)}, u32[]{:S(2)}) copy-start(f32[256]{0:T(256)} %param.22) | copy-start | bytes 3076
  16.4 72.2 %copy-start.1 = (bf16[256,1024]{1,0:T(8,128)(2,1)S(1)}, bf16[256,1024]{1,0:T(8,128)(2,1)}, u32[]{:S(2)}) copy-start(bf16[256,1024]{1,0:T(8,128)(2,1)} %param.23) | copy-start | bytes 1572868
  16.4 308.0 %reduce-scatter.7.cloned.1.call-start = ((), (), s32[]{:S(2)}) async-start(), calls=%async_computation.7 | async-start | bytes 5406720 | tf_op jit(solution)/shard_map/reduce_scatter | solution.py:39
  88.5 0.8 copy-start.2
  88.5 1.1 copy-start.3
  98.7 0.7 copy-start.7
  98.7 1.1 copy-start.8
  98.8 350.1 %all-reduce.6.cloned.1.call-start = ((), (), s32[]{:S(2)}) async-start(), calls=%async_computation.5 | async-start | bytes 2097152 | tf_op jit(solution)/shard_map/psum | solution.py:30
  325.7 2.3 copy-start.10
  328.9 51.6 %copy-start.11 = (bf16[1024,256]{1,0:T(8,128)(2,1)S(1)}, bf16[1024,256]{1,0:T(8,128)(2,1)}, u32[]{:S(2)}) copy-start(bf16[1024,256]{1,0:T(8,128)(2,1)} %param.26) | copy-start | bytes 1572868
  382.2 68.4 %copy-start.6 = (f32[256]{0:T(256)S(1)}, f32[256]{0:T(256)}, u32[]{:S(2)}) copy-start(f32[256]{0:T(256)} %param.27) | copy-start | bytes 3076
  382.2 305.2 %reduce-scatter.9.cloned.1.call-start = ((), (), s32[]{:S(2)}) async-start(), calls=%async_computation.8 | async-start | bytes 5406720 | tf_op jit(solution)/shard_map/reduce_scatter | solution.py:39
  450.6 1.9 copy-start.4
  450.6 2.2 copy-start.5
  461.9 430.6 %all-reduce.8.cloned.1.call-start = ((), (), s32[]{:S(2)}) async-start(), calls=%async_computation.6 | async-start | bytes 2097152 | tf_op jit(solution)/shard_map/psum | solution.py:30
  789.9 34.8 %copy-start.12 = (bf16[1024,256]{1,0:T(8,128)(2,1)S(1)}, bf16[1024,256]{1,0:T(8,128)(2,1)}, u32[]{:S(2)}) copy-start(bf16[1024,256]{1,0:T(8,128)(2,1)} %param.31) | copy-start | bytes 1572868
Sparse Core Ops, SparseCore 0:
  16.5 70.5 all-reduce.3
  98.9 225.4 reduce-scatter.6
  382.3 66.4 all-reduce.5
  462.0 225.3 reduce-scatter.8
  826.5 65.9 all-reduce.7
